TPU v7x, 32 devices: a whole 2x2x4 slice. The times are simulated.
32 devices in a mesh: section: 2 (over y), seq: 16 (over z, x, core).
Axes of the slice: x: 2, y: 2, z: 4, core: 2. Of those that a mesh axis runs over, the one named last changes fastest.
Arguments:
- queries: bfloat16 [2, 2048, 1024], P('section', 'seq'), may hold values from -35 to 35
- keys: bfloat16 [2, 2048, 1024], P('section', 'seq'), may hold values from -4 to 4
- values: bfloat16 [2, 2048, 1024], P('section', 'seq'), may hold values from -6 to 6
- upstream: bfloat16 [2, 2048, 1024], P('section', 'seq'), may hold values from -6 to 6
- neighbours: int32 [16, 6], replicated, may hold values from 0 to 15, as said below
- counts: int32 [16], replicated, may hold values from 1 to 6, as said below
Outputs:
- query_grad: bfloat16 [2, 2048, 1024], P('section', 'seq')
- key_grad: bfloat16 [2, 2048, 1024], P('section', 'seq')
- value_grad: bfloat16 [2, 2048, 1024], P('section', 'seq')
Inputs may be any that keep to these rules, and one draw needn't show every extreme that they name: Row a lists 6 different tiles, the first being a itself; only the first counts[a] of them are neighbours of a. `counts`: some tile has 6 neighbour tiles and some tile has only itself.
All inputs are finite; a program needn't handle non-finite values.
Results may differ from a plain program's by a relative error of at most 0.009.
Values may be sent and summed in bfloat16 or wider, within the bound.
A program may use at most 64 MiB of HBM per device.

v0:
```python
import jax
import jax.numpy as jnp
from jax import lax
from jax.sharding import PartitionSpec as P

HEADS = 16
DH = 64
TILE = 128
MAXNB = 6


MASKED = -1e30


def from_behind(block, axis, distance):
    devices = range(lax.axis_size(axis))
    route = [((i - distance) % len(devices), i) for i in devices]
    return lax.ppermute(block, axis, route)


def per_device(queries, keys, values, upstream, neighbours, counts):
    seq_count = lax.axis_size("seq")
    group_count = seq_count // HEADS
    row_count = queries.shape[1]
    model_width = queries.shape[2]
    quarter_rows = row_count // group_count
    unit_rows = min(quarter_rows, TILE)
    tile_count = neighbours.shape[0]
    my_group = lax.axis_index("seq") // HEADS
    adjoint = from_behind(upstream, "section", -1)

    def to_slots(block):
        return (
            block[0]
            .reshape(group_count, quarter_rows, HEADS, DH)
            .transpose(0, 2, 3, 1)
            .reshape(group_count * HEADS, DH, quarter_rows)
        )

    query_recv, adjoint_recv = (
        lax.all_to_all(to_slots(queries), "seq", split_axis=0, concat_axis=2, tiled=True),
        lax.all_to_all(to_slots(adjoint), "seq", split_axis=0, concat_axis=2, tiled=True),
    )
    query_cols = query_recv[0]
    adjoint_cols = adjoint_recv[0]

    def spread_rows(block):
        heads_first = block[0].reshape(row_count, HEADS, DH).transpose(1, 2, 0)
        return jnp.broadcast_to(heads_first[None], (group_count, HEADS, DH, row_count)).reshape(
            group_count * HEADS, DH, row_count
        )

    key_recv, value_recv = (
        lax.all_to_all(spread_rows(keys), "seq", split_axis=0, concat_axis=2, tiled=True),
        lax.all_to_all(spread_rows(values), "seq", split_axis=0, concat_axis=2, tiled=True),
    )
    key_cols = key_recv[0]
    value_cols = value_recv[0]
    key_tiles = key_cols.reshape(DH, tile_count, TILE).transpose(1, 0, 2)
    value_tiles = value_cols.reshape(DH, tile_count, TILE).transpose(1, 0, 2)
    query_total = seq_count * quarter_rows
    unit_count = query_total // unit_rows
    per_batch = min(unit_count, max(1, 512 // unit_rows))
    batch_count = unit_count // per_batch
    first_row = jnp.arange(unit_count, dtype=jnp.int32) * unit_rows
    source = first_row // quarter_rows
    offset = first_row % quarter_rows
    global_row = source * row_count + my_group * quarter_rows + offset
    unit_tiles = (global_row // TILE).reshape(batch_count, per_batch)

    def by_unit(cols):
        return cols.reshape(DH, batch_count, per_batch, unit_rows).transpose(1, 2, 0, 3)

    valid_table = (jnp.arange(MAXNB, dtype=jnp.int32)[None, :] < counts[:, None]).astype(
        jnp.float32
    )
    score_scale = DH ** (-0.5)
    tile_numbers = jnp.arange(tile_count, dtype=jnp.int32)

    def tile_sweep(carried, inputs):
        key_acc, value_acc = carried
        query_blk, adjoint_blk, tile_ids = inputs
        chosen = neighbours[tile_ids]
        alive_slots = valid_table[tile_ids][:, :, None, None]
        key_blk = key_tiles[chosen]
        value_blk = value_tiles[chosen]
        scores = (
            jnp.einsum("bei,bsej->bsij", query_blk, key_blk, preferred_element_type=jnp.float32)
            * score_scale
        )
        scores = jnp.where(alive_slots > 0, scores, MASKED)
        row_peak = jnp.max(scores, axis=(1, 3), keepdims=True)
        weights = jnp.exp(scores - row_peak) * alive_slots
        prob_full = weights / jnp.sum(weights, axis=(1, 3), keepdims=True)
        probs_low = prob_full.astype(jnp.bfloat16)
        dprobs = jnp.einsum(
            "bei,bsej->bsij", adjoint_blk, value_blk, preferred_element_type=jnp.float32
        )
        delta_sum = jnp.sum(prob_full * dprobs, axis=(1, 3), keepdims=True)
        dscores = (prob_full * (dprobs - delta_sum) * score_scale).astype(jnp.bfloat16)
        query_out = jnp.einsum(
            "bsij,bsej->bei", dscores, key_blk, preferred_element_type=jnp.float32
        ).astype(jnp.bfloat16)
        key_terms = jnp.einsum(
            "bsij,bei->bsej", dscores, query_blk, preferred_element_type=jnp.float32
        )
        value_terms = jnp.einsum(
            "bsij,bei->bsej", probs_low, adjoint_blk, preferred_element_type=jnp.float32
        )
        flat_ids = chosen.reshape(-1)
        picker = (flat_ids[None, :] == tile_numbers[:, None]).astype(jnp.float32)
        key_acc = key_acc + jnp.einsum(
            "tn,nej->tej",
            picker,
            key_terms.reshape(-1, DH, TILE),
            precision=lax.Precision.HIGHEST,
            preferred_element_type=jnp.float32,
        )
        value_acc = value_acc + jnp.einsum(
            "tn,nej->tej",
            picker,
            value_terms.reshape(-1, DH, TILE),
            precision=lax.Precision.HIGHEST,
            preferred_element_type=jnp.float32,
        )
        return ((key_acc, value_acc), query_out)

    empty_grad = jnp.zeros((tile_count, DH, TILE), jnp.float32)
    (key_acc, value_acc), query_units = lax.scan(
        tile_sweep,
        (empty_grad, empty_grad),
        (by_unit(query_cols), by_unit(adjoint_cols), unit_tiles),
    )
    query_send = (
        query_units.reshape(seq_count, quarter_rows // unit_rows, DH, unit_rows)
        .transpose(0, 2, 1, 3)
        .reshape(seq_count, 1, DH, quarter_rows)
    )
    query_back = lax.all_to_all(query_send, "seq", split_axis=0, concat_axis=1, tiled=True)
    query_grad = (
        query_back[0]
        .reshape(group_count, HEADS, DH, quarter_rows)
        .transpose(0, 3, 1, 2)
        .reshape(1, row_count, model_width)
    )

    def by_source(grad):
        return (
            grad.reshape(seq_count, row_count // TILE, DH, TILE)
            .transpose(0, 2, 1, 3)
            .reshape(seq_count, 1, DH, row_count)
        )

    got_key, got_value = (
        lax.all_to_all(
            by_source(key_acc).astype(jnp.bfloat16), "seq", split_axis=0, concat_axis=1, tiled=True
        ).astype(jnp.float32),
        lax.all_to_all(
            by_source(value_acc).astype(jnp.bfloat16),
            "seq",
            split_axis=0,
            concat_axis=1,
            tiled=True,
        ).astype(jnp.float32),
    )

    def finish_rows(got):
        summed = jnp.sum(got[0].reshape(group_count, HEADS, DH, row_count), axis=0)
        return summed.transpose(2, 0, 1).reshape(1, row_count, model_width).astype(jnp.bfloat16)

    key_grad = finish_rows(got_key)
    value_grad = finish_rows(got_value)
    return (query_grad, key_grad, value_grad)


def solution(mesh):
    in_specs = (
        P("section", "seq", None),
        P("section", "seq", None),
        P("section", "seq", None),
        P("section", "seq", None),
        P(),
        P(),
    )
    out_specs = (P("section", "seq", None), P("section", "seq", None), P("section", "seq", None))
    return jax.shard_map(
        per_device, mesh=mesh, in_specs=in_specs, out_specs=out_specs, check_vma=False
    )
```

profile of v0, /device:TPU:0, one launch (start us, length us, event | category | flops | bytes accessed | tf_op | source)
XLA Modules:
  0.0 162.7 jit_solution(16621503994922736800)
XLA Ops:
  0.7 1.8 %copy.46 = bf16[1,128,1024]{1,2,0:T(8,128)(2,1)} copy(bf16[1,128,1024]{2,1,0:T(8,128)(2,1)} %param.9) | data formatting | bytes 524288 | tf_op args[1]
  2.5 7.4 %all-to-all-start.1 = ((bf16[16,64,128]{2,1,0:T(8,128)(2,1)}), bf16[16,64,128]{2,1,0:T(8,128)(2,1)S(1)}, u32[]{:S(2)}, u32[]{:S(2)}) async-start(bf16[16,64,128]{2,1,0:T(8,128)(2,1)} %bitcast.8), calls=%async_computation.1 | async-start | bytes 524288 | tf_op jit(solution)/shard_map/all_to_all | solution.py:54
  9.9 1.8 %copy.47 = bf16[1,128,1024]{1,2,0:T(8,128)(2,1)} copy(bf16[1,128,1024]{2,1,0:T(8,128)(2,1)} %param.10) | data formatting | bytes 524288 | tf_op args[2]
  11.7 8.2 %all-to-all-done.1 = bf16[16,64,128]{2,1,0:T(8,128)(2,1)S(1)} async-done(((bf16[16,64,128]{2,1,0:T(8,128)(2,1)}), bf16[16,64,128]{2,1,0:T(8,128)(2,1)S(1)}, u32[]{:S(2)}, u32[]{:S(2)}) %all-to-all-start.1) | async-done | bytes 262176 | tf_op jit(solution)/shard_map/all_to_all | solution.py:54
  19.9 3.5 %all-to-all-start.2 = ((bf16[16,64,128]{2,1,0:T(8,128)(2,1)}), bf16[16,64,128]{2,1,0:T(8,128)(2,1)S(1)}, u32[]{:S(2)}, u32[]{:S(2)}) async-start(bf16[16,64,128]{2,1,0:T(8,128)(2,1)} %bitcast.10), calls=%async_computation.2 | async-start | bytes 524288 | tf_op jit(solution)/shard_map/all_to_all | solution.py:55
  23.5 0.8 copy.45
  24.3 9.1 %all-to-all-done.2 = bf16[16,64,128]{2,1,0:T(8,128)(2,1)S(1)} async-done(((bf16[16,64,128]{2,1,0:T(8,128)(2,1)}), bf16[16,64,128]{2,1,0:T(8,128)(2,1)S(1)}, u32[]{:S(2)}, u32[]{:S(2)}) %all-to-all-start.2) | async-done | bytes 262176 | tf_op jit(solution)/shard_map/all_to_all | solution.py:55
  33.4 3.5 %all-to-all-start = ((bf16[16,64,128]{2,1,0:T(8,128)(2,1)}), bf16[16,64,128]{2,1,0:T(8,128)(2,1)S(1)}, u32[]{:S(2)}, u32[]{:S(2)}) async-start(bf16[16,64,128]{2,1,0:T(8,128)(2,1)} %bitcast.2), calls=%async_computation | async-start | bytes 524288 | tf_op jit(solution)/shard_map/all_to_all | solution.py:41
  37.2 1.6 collective-permute-start
  38.7 7.1 %collective-permute-done = bf16[1,128,1024]{1,2,0:T(8,128)(2,1)} collective-permute-done((bf16[1,128,1024]{1,2,0:T(8,128)(2,1)S(1)}, bf16[1,128,1024]{1,2,0:T(8,128)(2,1)}, u32[]{:S(2)}, u32[]{:S(2)}) %collective-permute-start) | collective-permute-done | bytes 262176 | tf_op jit(solution)/shard_map/ppermute | solution.py:18
  45.8 1.1 all-to-all-done
  46.9 4.7 %all-to-all-start.3 = ((bf16[16,64,128]{2,1,0:T(8,128)(2,1)}), bf16[16,64,128]{2,1,0:T(8,128)(2,1)}, u32[]{:S(2)}, u32[]{:S(2)}) async-start(bf16[16,64,128]{2,1,0:T(8,128)(2,1)} %bitcast.13), calls=%async_computation.3 | async-start | bytes 524288 | tf_op jit(solution)/shard_map/all_to_all | solution.py:42
  52.4 9.3 %all-to-all-done.3 = bf16[16,64,128]{2,1,0:T(8,128)(2,1)} async-done(((bf16[16,64,128]{2,1,0:T(8,128)(2,1)}), bf16[16,64,128]{2,1,0:T(8,128)(2,1)}, u32[]{:S(2)}, u32[]{:S(2)}) %all-to-all-start.3) | async-done | bytes 262176 | tf_op jit(solution)/shard_map/all_to_all | solution.py:42
  61.8 58.4 %while.15 = (s32[]{:T(128)}, f32[16,64,128]{2,0,1:T(8,128)}, f32[16,64,128]{2,0,1:T(8,128)}, bf16[4,4,64,128]{3,2,1,0:T(8,128)(2,1)}, s32[4,4]{1,0:T(4,128)}, /*...) while((s32[]{:T(128)}, f32[16,64,128]{2,0,1:T(8,128)}, ...), condition=%wide.region_4.5_spmd.clone, body=%wide.region_0.4_spmd.clone.sunk | while | flops 336365120 | bytes 25971868 | solution.py:129
  61.8 0.7 fusion.88
  63.1 0.6 gather_fusion.1
  63.8 0.7 fusion.89
  66.0 1.3 fusion.94
  67.3 0.6 eq.43
  67.9 2.3 %convolution_add_fusion.5 = f32[16,64,128]{2,0,1:T(8,128)} fusion(f32[24,64,128]{2,1,0:T(8,128)S(1)} %bitcast.200, f32[16,64,128]{2,0,1:T(8,128)} %get-tuple-element.266, pred[]{:T(512)S(6)} %compare.14, s32[24]{0:T(128)} %eq.43), kind=kOutput, calls=%fused_computation.19.clone.1 | convolution fusion | flops 38011264 | bytes 1835105 | tf_op jit(solution)/shard_map/while/body/eval_jaxpr/tn,nej->tej/dot_general | solution.py:119
  70.2 0.7 gather_fusion.3
  71.0 1.5 fusion.91
  73.5 0.6 copy-done
  74.2 1.0 convolution_add_fusion.4
  75.1 0.9 fusion.95
  76.0 0.7 fusion.88
  77.4 0.6 gather_fusion.1
  78.0 0.7 fusion.89
  80.2 1.3 fusion.94
  82.2 2.7 %convolution_add_fusion.5 = f32[16,64,128]{2,0,1:T(8,128)} fusion(f32[24,64,128]{2,1,0:T(8,128)S(1)} %bitcast.200, f32[16,64,128]{2,0,1:T(8,128)} %get-tuple-element.266, pred[]{:T(512)S(6)} %compare.14, s32[24]{0:T(128)} %eq.43), kind=kOutput, calls=%fused_computation.19.clone.1 | convolution fusion | flops 38011264 | bytes 1835105 | tf_op jit(solution)/shard_map/while/body/eval_jaxpr/tn,nej->tej/dot_general | solution.py:119
  84.9 0.7 gather_fusion.3
  85.7 1.5 fusion.91
  88.2 0.6 copy-done
  88.9 1.0 convolution_add_fusion.4
  89.8 0.9 fusion.95
  90.8 0.7 fusion.88
  92.1 0.6 gather_fusion.1
  92.8 0.7 fusion.89
  95.0 1.3 fusion.94
  96.9 2.7 %convolution_add_fusion.5 = f32[16,64,128]{2,0,1:T(8,128)} fusion(f32[24,64,128]{2,1,0:T(8,128)S(1)} %bitcast.200, f32[16,64,128]{2,0,1:T(8,128)} %get-tuple-element.266, pred[]{:T(512)S(6)} %compare.14, s32[24]{0:T(128)} %eq.43), kind=kOutput, calls=%fused_computation.19.clone.1 | convolution fusion | flops 38011264 | bytes 1835105 | tf_op jit(solution)/shard_map/while/body/eval_jaxpr/tn,nej->tej/dot_general | solution.py:119
  99.7 0.7 gather_fusion.3
  100.4 1.5 fusion.91
  103.0 0.6 copy-done
  103.6 1.0 convolution_add_fusion.4
  104.6 0.9 fusion.95
  105.5 0.7 fusion.88
  106.8 0.6 gather_fusion.1
  107.5 0.7 fusion.89
  109.7 1.3 fusion.94
  111.7 2.7 %convolution_add_fusion.5 = f32[16,64,128]{2,0,1:T(8,128)} fusion(f32[24,64,128]{2,1,0:T(8,128)S(1)} %bitcast.200, f32[16,64,128]{2,0,1:T(8,128)} %get-tuple-element.266, pred[]{:T(512)S(6)} %compare.14, s32[24]{0:T(128)} %eq.43), kind=kOutput, calls=%fused_computation.19.clone.1 | convolution fusion | flops 38011264 | bytes 1835105 | tf_op jit(solution)/shard_map/while/body/eval_jaxpr/tn,nej->tej/dot_general | solution.py:119
  114.4 0.7 gather_fusion.3
  115.1 1.5 fusion.91
  117.7 0.6 copy-done
  118.3 1.0 convolution_add_fusion.4
  119.3 0.9 fusion.95
  120.2 2.0 %copy.71 = bf16[16,64,128]{2,1,0:T(8,128)(2,1)} copy(f32[16,64,128]{2,0,1:T(8,128)} %get-tuple-element.68) | data formatting | bytes 786432 | tf_op jit(solution)/shard_map/while | solution.py:129
  122.2 3.5 %all-to-all-start.5 = ((bf16[16,1,64,128]{3,2,1,0:T(8,128)(2,1)}), bf16[16,1,64,128]{3,2,1,0:T(8,128)(2,1)S(1)}, u32[]{:S(2)}, u32[]{:S(2)}) async-start(bf16[16,1,64,128]{3,2,1,0:T(8,128)(2,1)} %bitcast.141), calls=%async_computation.5 | async-start | bytes 524288 | tf_op jit(solution)/shard_map/all_to_all | solution.py:155
  125.9 9.8 %all-to-all-done.5 = bf16[16,1,64,128]{3,2,1,0:T(8,128)(2,1)S(1)} async-done(((bf16[16,1,64,128]{3,2,1,0:T(8,128)(2,1)}), bf16[16,1,64,128]{3,2,1,0:T(8,128)(2,1)S(1)}, u32[]{:S(2)}, u32[]{:S(2)}) %all-to-all-start.5) | async-done | bytes 262176 | tf_op jit(solution)/shard_map/all_to_all | solution.py:155
  135.7 12.7 %all_to_all.78 = bf16[16,1,64,128]{3,2,1,0:T(8,128)(2,1)S(1)} all-to-all(bf16[16,1,64,128]{3,2,1,0:T(8,128)(2,1)S(1)} %bitcast.203), channel_id=1, replica_groups=mesh['section'=2,'seq'=16] {'seq'}, dimensions={0} | all-to-all | bytes 524288 | tf_op jit(solution)/shard_map/all_to_all | solution.py:158
  148.4 3.5 %all-to-all-start.4 = ((bf16[16,1,64,128]{3,2,1,0:T(8,128)(2,1)}), bf16[16,1,64,128]{3,2,1,0:T(8,128)(2,1)S(1)}, u32[]{:S(2)}, u32[]{:S(2)}) async-start(bf16[16,1,64,128]{3,2,1,0:T(8,128)(2,1)} %bitcast.18), calls=%async_computation.4 | async-start | bytes 524288 | tf_op jit(solution)/shard_map/all_to_all | solution.py:139
  151.9 0.9 copy.53
  152.8 0.8 copy.54
  153.6 8.3 %all-to-all-done.4 = bf16[16,1,64,128]{3,2,1,0:T(8,128)(2,1)S(1)} async-done(((bf16[16,1,64,128]{3,2,1,0:T(8,128)(2,1)}), bf16[16,1,64,128]{3,2,1,0:T(8,128)(2,1)S(1)}, u32[]{:S(2)}, u32[]{:S(2)}) %all-to-all-start.4) | async-done | bytes 262176 | tf_op jit(solution)/shard_map/all_to_all | solution.py:139
  161.9 0.8 copy.52
  (122 shorter events, 15.4 us)
Async XLA Ops:
  0.6 22.8 %copy-start.6 = (bf16[1,128,1024]{2,1,0:T(8,128)(2,1)S(1)}, bf16[1,128,1024]{2,1,0:T(8,128)(2,1)}, u32[]{:S(2)}) copy-start(bf16[1,128,1024]{2,1,0:T(8,128)(2,1)} %param.8) | copy-start | bytes 786436
  0.6 36.3 %copy-start.7 = (bf16[1,128,1024]{2,1,0:T(8,128)(2,1)S(1)}, bf16[1,128,1024]{2,1,0:T(8,128)(2,1)}, u32[]{:S(2)}) copy-start(bf16[1,128,1024]{2,1,0:T(8,128)(2,1)} %param.11) | copy-start | bytes 786436
  2.5 17.4 %all-to-all-start.1 = ((bf16[16,64,128]{2,1,0:T(8,128)(2,1)}), bf16[16,64,128]{2,1,0:T(8,128)(2,1)S(1)}, u32[]{:S(2)}, u32[]{:S(2)}) async-start(bf16[16,64,128]{2,1,0:T(8,128)(2,1)} %bitcast.8), calls=%async_computation.1 | async-start | bytes 524288 | tf_op jit(solution)/shard_map/all_to_all | solution.py:54
  9.9 41.8 %copy-start.11 = (s32[16,6]{0,1:T(8,128)S(1)}, s32[16,6]{0,1:T(8,128)}, u32[]{:S(2)}) copy-start(s32[16,6]{0,1:T(8,128)} %param.12) | copy-start | bytes 1156
  19.9 13.5 %all-to-all-start.2 = ((bf16[16,64,128]{2,1,0:T(8,128)(2,1)}), bf16[16,64,128]{2,1,0:T(8,128)(2,1)S(1)}, u32[]{:S(2)}, u32[]{:S(2)}) async-start(bf16[16,64,128]{2,1,0:T(8,128)(2,1)} %bitcast.10), calls=%async_computation.2 | async-start | bytes 524288 | tf_op jit(solution)/shard_map/all_to_all | solution.py:55
  33.4 13.5 %all-to-all-start = ((bf16[16,64,128]{2,1,0:T(8,128)(2,1)}), bf16[16,64,128]{2,1,0:T(8,128)(2,1)S(1)}, u32[]{:S(2)}, u32[]{:S(2)}) async-start(bf16[16,64,128]{2,1,0:T(8,128)(2,1)} %bitcast.2), calls=%async_computation | async-start | bytes 524288 | tf_op jit(solution)/shard_map/all_to_all | solution.py:41
  37.2 8.7 %collective-permute-start = (bf16[1,128,1024]{1,2,0:T(8,128)(2,1)S(1)}, bf16[1,128,1024]{1,2,0:T(8,128)(2,1)}, u32[]{:S(2)}, u32[]{:S(2)}) collective-permute-start(bf16[1,128,1024]{1,2,0:T(8,128)(2,1)S(1)} %copy.48), channel_id=1, source_target_pairs={{16,0},{0,16},{17,1},{1,17},{18,2},{2,18},{19,3},{3,19},{20,4},{4,... | collective-permute-start | bytes 786440 | tf_op jit(solution)/shard_map/ppermute | solution.py:18
  46.9 14.8 %all-to-all-start.3 = ((bf16[16,64,128]{2,1,0:T(8,128)(2,1)}), bf16[16,64,128]{2,1,0:T(8,128)(2,1)}, u32[]{:S(2)}, u32[]{:S(2)}) async-start(bf16[16,64,128]{2,1,0:T(8,128)(2,1)} %bitcast.13), calls=%async_computation.3 | async-start | bytes 524288 | tf_op jit(solution)/shard_map/all_to_all | solution.py:42
  63.1 0.6 copy-start.5
  65.6 1.7 %copy-start.3 = (f32[4,128]{1,0:T(4,128)}, f32[4,128]{1,0:T(4,128)S(1)}, u32[]{:S(2)}) copy-start(f32[4,128]{1,0:T(4,128)S(1)} %get-tuple-element.248) | copy-start | bytes 6148 | tf_op jit(solution)/shard_map/while
  66.0 1.4 copy-start.8
  67.9 3.0 %copy-start.4 = (f32[4,128]{1,0:T(4,128)S(1)}, f32[4,128]{1,0:T(4,128)}, u32[]{:S(2)}) copy-start(f32[4,128]{1,0:T(4,128)} %copy-done.3) | copy-start | bytes 6148 | tf_op jit(solution)/shard_map/while
  71.0 1.5 copy-start.9
  73.1 1.0 copy-start
  73.1 1.0 copy-start.10
  75.1 0.9 copy-start.1
  77.4 0.6 copy-start.5
  79.9 1.7 %copy-start.3 = (f32[4,128]{1,0:T(4,128)}, f32[4,128]{1,0:T(4,128)S(1)}, u32[]{:S(2)}) copy-start(f32[4,128]{1,0:T(4,128)S(1)} %get-tuple-element.248) | copy-start | bytes 6148 | tf_op jit(solution)/shard_map/while
  80.2 1.4 copy-start.8
  82.2 3.5 %copy-start.4 = (f32[4,128]{1,0:T(4,128)S(1)}, f32[4,128]{1,0:T(4,128)}, u32[]{:S(2)}) copy-start(f32[4,128]{1,0:T(4,128)} %copy-done.3) | copy-start | bytes 6148 | tf_op jit(solution)/shard_map/while
  85.7 1.5 copy-start.9
  87.8 1.0 copy-start
  87.8 1.0 copy-start.10
  89.8 0.9 copy-start.1
  92.1 0.6 copy-start.5
  94.6 1.7 %copy-start.3 = (f32[4,128]{1,0:T(4,128)}, f32[4,128]{1,0:T(4,128)S(1)}, u32[]{:S(2)}) copy-start(f32[4,128]{1,0:T(4,128)S(1)} %get-tuple-element.248) | copy-start | bytes 6148 | tf_op jit(solution)/shard_map/while
  95.0 1.4 copy-start.8
  96.9 3.5 %copy-start.4 = (f32[4,128]{1,0:T(4,128)S(1)}, f32[4,128]{1,0:T(4,128)}, u32[]{:S(2)}) copy-start(f32[4,128]{1,0:T(4,128)} %copy-done.3) | copy-start | bytes 6148 | tf_op jit(solution)/shard_map/while
  100.4 1.5 copy-start.9
  102.5 1.0 copy-start
  102.6 1.0 copy-start.10
  104.5 0.9 copy-start.1
  106.8 0.6 copy-start.5
  109.3 1.7 %copy-start.3 = (f32[4,128]{1,0:T(4,128)}, f32[4,128]{1,0:T(4,128)S(1)}, u32[]{:S(2)}) copy-start(f32[4,128]{1,0:T(4,128)S(1)} %get-tuple-element.248) | copy-start | bytes 6148 | tf_op jit(solution)/shard_map/while
  109.7 1.4 copy-start.8
  111.7 3.5 %copy-start.4 = (f32[4,128]{1,0:T(4,128)S(1)}, f32[4,128]{1,0:T(4,128)}, u32[]{:S(2)}) copy-start(f32[4,128]{1,0:T(4,128)} %copy-done.3) | copy-start | bytes 6148 | tf_op jit(solution)/shard_map/while
  115.1 1.5 copy-start.9
  117.3 1.0 copy-start
  117.3 1.0 copy-start.10
  119.3 0.9 copy-start.1
  120.2 5.5 %copy-start.2 = (f32[16,64,128]{2,0,1:T(8,128)S(1)}, f32[16,64,128]{2,0,1:T(8,128)}, u32[]{:S(2)}) copy-start(f32[16,64,128]{2,0,1:T(8,128)} %get-tuple-element.69) | copy-start | bytes 1572868
  122.2 13.5 %all-to-all-start.5 = ((bf16[16,1,64,128]{3,2,1,0:T(8,128)(2,1)}), bf16[16,1,64,128]{3,2,1,0:T(8,128)(2,1)S(1)}, u32[]{:S(2)}, u32[]{:S(2)}) async-start(bf16[16,1,64,128]{3,2,1,0:T(8,128)(2,1)} %bitcast.141), calls=%async_computation.5 | async-start | bytes 524288 | tf_op jit(solution)/shard_map/all_to_all | solution.py:155
  148.4 13.5 %all-to-all-start.4 = ((bf16[16,1,64,128]{3,2,1,0:T(8,128)(2,1)}), bf16[16,1,64,128]{3,2,1,0:T(8,128)(2,1)S(1)}, u32[]{:S(2)}, u32[]{:S(2)}) async-start(bf16[16,1,64,128]{3,2,1,0:T(8,128)(2,1)} %bitcast.18), calls=%async_computation.4 | async-start | bytes 524288 | tf_op jit(solution)/shard_map/all_to_all | solution.py:139
where the time goes:
time: 164 us; the launch traced here: 163 us
  waiting for transfers between devices  52.9 us (32%)
  matrix products  33 us (20%)
  starting transfers between devices  27.8 us (17%)
  local copies, waits for them, and re-layouts  24.8 us (15%)
  blocking collectives  12.7 us (8%)
  other arithmetic  10.2 us (6%)
    all_to_all x1, blocking collectives, per_device(): lax.all_to_all(by_source(value_acc).astype(jnp.bfloat16), 'seq', split_ax...  12.7 us
    dot_general x4, matrix products, tile_sweep(): jnp.einsum('tn,nej->tej', picker, value_terms.reshape(-1, DH, TILE), prec...  10.4 us
    all_to_all x1, waiting for transfers between devices, per_device(): lax.all_to_all(by_source(key_acc).astype(jnp.bfloat16), 'seq', split_axis...  9.79 us
    all_to_all x1, waiting for transfers between devices, per_device(): lax.all_to_all(to_slots(adjoint), 'seq', split_axis=0, concat_axis=2, til...  9.33 us
    all_to_all x1, waiting for transfers between devices, per_device(): lax.all_to_all(spread_rows(values), 'seq', split_axis=0, concat_axis=2, t...  9.13 us
    all_to_all x1, waiting for transfers between devices, per_device(): lax.all_to_all(query_send, 'seq', split_axis=0, concat_axis=1, tiled=True)  8.28 us
    all_to_all x1, waiting for transfers between devices, per_device(): lax.all_to_all(spread_rows(keys), 'seq', split_axis=0, concat_axis=2, til...  8.21 us
    all_to_all x1, starting transfers between devices, per_device(): lax.all_to_all(spread_rows(keys), 'seq', split_axis=0, concat_axis=2, til...  7.39 us
  transfers between devices with their start and end apart: 7, of which 7 were waited for; matrix products, arithmetic and copies ran while one was open for 3% of the time, Pallas kernels for 0%

commit v1 on v0

v1 whole, which is shorter than its diff:
```python
import functools
import math

import jax
import jax.numpy as jnp
from jax import lax
from jax.experimental import pallas as pl
from jax.experimental.pallas import tpu as pltpu
from jax.sharding import PartitionSpec as P

HEADS = 16
DH = 64
TILE = 128
MAXNB = 6
MASKED = -1e30
MESH = pl.DeviceIdType.MESH
EXPONENT = DH ** (-0.5) * math.log2(math.e)
NT = (((1,), (1,)), ((), ()))


def kernel(
    sections,
    tiles,
    near_ref,
    count_ref,
    q_ref,
    k_ref,
    v_ref,
    u_ref,
    dq_ref,
    dk_ref,
    dv_ref,
    q_send,
    k_send,
    v_send,
    u_send,
    q_got,
    k_got,
    v_got,
    u_got,
    k_rows,
    v_rows,
    ds_all,
    pr_all,
    dq_send,
    dk_send,
    dv_send,
    dq_got,
    dk_got,
    dv_got,
    slot_ref,
    send_sem,
    recv_sem,
    q_sem,
    u_sem,
):
    section = lax.axis_index("section")
    me = lax.axis_index("seq")
    group = me // HEADS
    head = me % HEADS
    behind = lax.rem(section + sections - 1, sections)
    ahead = lax.rem(section + 1, sections)
    pairs = HEADS * MAXNB

    barrier = pltpu.get_barrier_semaphore()

    def greet(r, c):
        pl.semaphore_signal(
            barrier, inc=1, device_id=(section, lax.rem(me + r, tiles)), device_id_type=MESH
        )
        return c

    def greet_ahead(h, c):
        pl.semaphore_signal(
            barrier, inc=1, device_id=(ahead, group * HEADS + h), device_id_type=MESH
        )
        return c

    lax.fori_loop(1, tiles, greet, 0)
    lax.fori_loop(0, HEADS, greet_ahead, 0)

    def turn(src, dst):
        for c in range(HEADS // 2):
            flipped = src[:, c * 128 : (c + 1) * 128].T
            dst[2 * c] = flipped[:DH]
            dst[2 * c + 1] = flipped[DH:]

    turn(k_ref, k_send)
    turn(v_ref, v_send)
    turn(q_ref, q_send)
    turn(u_ref, u_send)
    pl.semaphore_wait(barrier, tiles - 1 + HEADS)

    def remote(src, dst, sent, got, where, peer):
        return pltpu.make_async_remote_copy(
            src_ref=src,
            dst_ref=dst,
            send_sem=sent,
            recv_sem=got,
            device_id=(where, peer),
            device_id_type=MESH,
        )

    def send_kv(r, c):
        peer = lax.rem(me + r, tiles)
        block = peer % HEADS
        remote(
            k_send.at[block], k_got.at[me], send_sem.at[0], recv_sem.at[0], section, peer
        ).start()
        remote(
            v_send.at[block], v_got.at[me], send_sem.at[1], recv_sem.at[1], section, peer
        ).start()
        return c

    lax.fori_loop(1, tiles, send_kv, 0)

    def send_qu(r, c):
        h = lax.rem(head + r, HEADS)
        peer = group * HEADS + h
        remote(
            q_send.at[h], q_got.at[head], send_sem.at[2], q_sem.at[head], section, peer
        ).start()
        remote(
            u_send.at[h], u_got.at[head], send_sem.at[3], u_sem.at[head], behind, peer
        ).start()
        return c

    remote(
        u_send.at[head], u_got.at[head], send_sem.at[3], u_sem.at[head], behind, me
    ).start()
    lax.fori_loop(1, HEADS, send_qu, 0)

    k_got[me] = k_send[head]
    v_got[me] = v_send[head]
    q_got[head] = q_send[head]
    ds_all[pairs] = jnp.zeros((TILE, TILE), jnp.bfloat16)
    pr_all[pairs] = jnp.zeros((TILE, TILE), jnp.bfloat16)

    def find(a, c):
        tile = group * HEADS + a
        live = count_ref[tile]
        listed = [
            jnp.where(s < live, near_ref[tile, s], -1) for s in range(MAXNB)
        ]

        def one(b, c):
            found = jnp.int32(pairs)
            for s in range(MAXNB):
                found = jnp.where(listed[s] == b, a * MAXNB + s, found)
            slot_ref[b, a] = found
            return c

        return lax.fori_loop(0, tiles, one, c)

    lax.fori_loop(0, HEADS, find, 0)

    def settle(buffer, count, semaphore):
        part = buffer.at[pl.ds(0, count)]
        pltpu.make_async_copy(part, part, semaphore).wait()

    settle(k_got, tiles - 1, recv_sem.at[0])
    settle(v_got, tiles - 1, recv_sem.at[1])

    def upright(b, c):
        k_rows[b] = k_got[b].T
        v_rows[b] = v_got[b].T
        return c

    lax.fori_loop(0, tiles, upright, 0)

    def query_tile(a):
        tile = group * HEADS + a
        live = count_ref[tile]
        query = q_got[a]
        adjoint = u_got[a]
        near = [near_ref[tile, s] for s in range(MAXNB)]
        scores = []
        for s in range(MAXNB):
            raw = jnp.dot(k_rows[near[s]], query, preferred_element_type=jnp.float32)
            scores.append(jnp.where(s < live, raw, MASKED) if s else raw)
        peak = functools.reduce(
            jnp.maximum, [jnp.max(raw, axis=0, keepdims=True) for raw in scores]
        )
        weights = [jnp.exp2((raw - peak) * EXPONENT) for raw in scores]
        total = sum(jnp.sum(w, axis=0, keepdims=True) for w in weights)
        share = 1.0 / total
        dprobs = [
            jnp.dot(v_rows[near[s]], adjoint, preferred_element_type=jnp.float32)
            for s in range(MAXNB)
        ]
        delta = share * sum(
            jnp.sum(w * d, axis=0, keepdims=True) for w, d in zip(weights, dprobs)
        )
        scaled = share * (DH ** (-0.5))
        out = jnp.zeros((DH, TILE), jnp.float32)
        for s in range(MAXNB):
            pr_all[a * MAXNB + s] = (weights[s] * share).astype(jnp.bfloat16)
            dscore = ((weights[s] * scaled) * (dprobs[s] - delta)).astype(jnp.bfloat16)
            ds_all[a * MAXNB + s] = dscore
            out += jnp.dot(k_got[near[s]], dscore, preferred_element_type=jnp.float32)
        dq_send[a] = out.astype(jnp.bfloat16)

    def await_u(a):
        pltpu.make_async_copy(u_got.at[a], u_got.at[a], u_sem.at[a]).wait()

    await_u(head)
    query_tile(head)
    dq_got[head] = dq_send[head]

    def query_step(r, c):
        a = lax.rem(head + HEADS - r, HEADS)
        pltpu.make_async_copy(q_got.at[a], q_got.at[a], q_sem.at[a]).wait()
        await_u(a)
        query_tile(a)
        remote(
            dq_send.at[a],
            dq_got.at[head],
            send_sem.at[4],
            recv_sem.at[2],
            section,
            group * HEADS + a,
        ).start()
        return c

    lax.fori_loop(1, HEADS, query_step, 0)

    def key_tile(b):
        key_sum = jnp.zeros((DH, TILE), jnp.float32)
        value_sum = jnp.zeros((DH, TILE), jnp.float32)
        for a in range(HEADS):
            slot = slot_ref[b, a]
            key_sum += lax.dot_general(
                q_got[a], ds_all[slot], NT, preferred_element_type=jnp.float32
            )
            value_sum += lax.dot_general(
                u_got[a], pr_all[slot], NT, preferred_element_type=jnp.float32
            )
        dk_send[b] = key_sum.astype(jnp.bfloat16)
        dv_send[b] = value_sum.astype(jnp.bfloat16)

    def key_step(r, c):
        b = lax.rem(me + r, tiles)
        key_tile(b)
        remote(
            dk_send.at[b], dk_got.at[me], send_sem.at[5], recv_sem.at[3], section, b
        ).start()
        remote(
            dv_send.at[b], dv_got.at[me], send_sem.at[6], recv_sem.at[4], section, b
        ).start()
        return c

    lax.fori_loop(1, tiles, key_step, 0)
    key_tile(me)
    dk_got[me] = dk_send[me]
    dv_got[me] = dv_send[me]

    def unturn(src, dst):
        for c in range(HEADS // 2):
            parts = []
            for h in (2 * c, 2 * c + 1):
                if tiles == HEADS or src is dq_got:
                    parts.append(src[h])
                else:
                    parts.append(
                        sum(
                            src[g * HEADS + h].astype(jnp.float32)
                            for g in range(tiles // HEADS)
                        ).astype(jnp.bfloat16)
                    )
            dst[:, c * 128 : (c + 1) * 128] = jnp.concatenate(parts, axis=0).T

    settle(dq_got, HEADS - 1, recv_sem.at[2])
    unturn(dq_got, dq_ref)
    settle(dk_got, tiles - 1, recv_sem.at[3])
    unturn(dk_got, dk_ref)
    settle(dv_got, tiles - 1, recv_sem.at[4])
    unturn(dv_got, dv_ref)

    settle(k_got, tiles - 1, send_sem.at[0])
    settle(v_got, tiles - 1, send_sem.at[1])
    settle(q_got, HEADS - 1, send_sem.at[2])
    settle(u_got, HEADS, send_sem.at[3])
    settle(dq_got, HEADS - 1, send_sem.at[4])
    settle(dk_got, tiles - 1, send_sem.at[5])
    settle(dv_got, tiles - 1, send_sem.at[6])


def per_device(queries, keys, values, upstream, neighbours, counts):
    sections = lax.axis_size("section")
    tiles = lax.axis_size("seq")
    rows, width = queries.shape[1:]
    assert rows == TILE and width == HEADS * DH and tiles % HEADS == 0
    vmem = pl.BlockSpec(memory_space=pltpu.VMEM)
    smem = pl.BlockSpec(memory_space=pltpu.SMEM)
    out = jax.ShapeDtypeStruct((rows, width), jnp.bfloat16)

    def blocks(count):
        return pltpu.VMEM((count, DH, TILE), jnp.bfloat16)

    pairs = HEADS * MAXNB + 1
    dq, dk, dv = pl.pallas_call(
        functools.partial(kernel, sections, tiles),
        out_shape=(out, out, out),
        in_specs=[smem, smem, vmem, vmem, vmem, vmem],
        out_specs=(vmem, vmem, vmem),
        scratch_shapes=[blocks(HEADS)] * 4
        + [blocks(HEADS), blocks(tiles), blocks(tiles), blocks(HEADS)]
        + [pltpu.VMEM((tiles, TILE, DH), jnp.bfloat16)] * 2
        + [pltpu.VMEM((pairs, TILE, TILE), jnp.bfloat16)] * 2
        + [blocks(HEADS), blocks(tiles), blocks(tiles)]
        + [blocks(HEADS), blocks(tiles), blocks(tiles)]
        + [
            pltpu.SMEM((tiles, HEADS), jnp.int32),
            pltpu.SemaphoreType.DMA((7,)),
            pltpu.SemaphoreType.DMA((5,)),
            pltpu.SemaphoreType.DMA((HEADS,)),
            pltpu.SemaphoreType.DMA((HEADS,)),
        ],
        compiler_params=pltpu.CompilerParams(
            collective_id=0, has_side_effects=True, vmem_limit_bytes=60 * 1024 * 1024
        ),
    )(neighbours, counts, queries[0], keys[0], values[0], upstream[0])
    return dq[None], dk[None], dv[None]


def solution(mesh):
    spec = P("section", "seq", None)
    return jax.shard_map(
        per_device,
        mesh=mesh,
        in_specs=(spec, spec, spec, spec, P(), P()),
        out_specs=(spec, spec, spec),
        check_vma=False,
    )
```

time: 164 us -> 61 us (0.37)
  the two profiles are of different devices: /device:TPU:0 before, /device:TPU:11 now
where the time goes in v1:
time: 61 us; the launch traced here: 60.5 us
  Pallas kernels  55 us (90%)
  local copies, waits for them, and re-layouts  4.82 us (8%)
  between operations  0.66 us (1%)
    pallas_call x1, Pallas kernels, per_device(): pl.pallas_call(functools.partial(kernel, sections, tiles), out_shape=(out...  55 us
    unnamed x10, local copies, waits for them, and re-layouts  4.82 us

profile of v1, /device:TPU:11, one launch (start us, length us, event | category | flops | bytes accessed | tf_op | source)
XLA Modules:
  0.0 60.5 jit_solution(3110625090137213509)
XLA Ops:
  0.6 0.0 copy-start.2
  0.6 0.7 %copy-done.2 = s32[16,6]{0,1:T(8,128)S(1)} copy-done((s32[16,6]{0,1:T(8,128)S(1)}, s32[16,6]{0,1:T(8,128)}, u32[]{:S(2)}) %copy-start.2) | copy-done | bytes 408
  1.3 0.7 %copy.9.near_ref = s32[16,6]{1,0:T(8,128)} copy(s32[16,6]{0,1:T(8,128)S(1)} %copy-done.2) | data formatting | bytes 768 | tf_op args[4]
  2.0 55.0 %shard_map.85 = (bf16[128,1024]{1,0:T(8,128)(2,1)}, bf16[128,1024]{1,0:T(8,128)(2,1)}, bf16[128,1024]{1,0:T(8,128)(2,1)}) custom-call(s32[16,6]{1,0:T(8,128)} %copy.9.near_ref, s32[16]{0:T(128)} %count_ref.1, bf16[128,1024]{1,0:T(8,128)(2,1)} %bitcast.10, bf16[128,1024]{1,0:T(8,128)(2,1)} %bitcast.11, bf16[128,1024]{1,0:T(8,128)(2,1)} %bitcast.12, ...), custom_call_target="tpu_custom_call" | custom-call | tf_op jit(solution)/shard_map/pallas_call | solution.py:301
  57.0 0.0 copy-start.1
  57.0 1.7 %copy.13 = bf16[1,128,1024]{2,1,0:T(8,128)(2,1)} copy(bf16[1,128,1024]{2,1,0:T(8,128)(2,1)} %bitcast.9) | data formatting | bytes 524288
  58.7 0.0 copy-done.1
  58.7 0.0 copy-start
  58.7 0.7 %copy.14 = bf16[1,128,1024]{2,1,0:T(8,128)(2,1)} copy(bf16[1,128,1024]{2,1,0:T(8,128)(2,1)S(1)} %bitcast.8) | data formatting | bytes 524288
  59.4 0.3 copy-done
  59.8 0.7 %copy.15 = bf16[1,128,1024]{2,1,0:T(8,128)(2,1)} copy(bf16[1,128,1024]{2,1,0:T(8,128)(2,1)S(1)} %bitcast.7) | data formatting | bytes 524288
Async XLA Ops:
  0.6 0.7 %copy-start.2 = (s32[16,6]{0,1:T(8,128)S(1)}, s32[16,6]{0,1:T(8,128)}, u32[]{:S(2)}) copy-start(s32[16,6]{0,1:T(8,128)} %param.10) | copy-start | bytes 1156
  57.0 1.7 %copy-start.1 = (bf16[128,1024]{1,0:T(8,128)(2,1)S(1)}, bf16[128,1024]{1,0:T(8,128)(2,1)}, u32[]{:S(2)}) copy-start(bf16[128,1024]{1,0:T(8,128)(2,1)} %get-tuple-element.7) | copy-start | bytes 786436
  58.7 1.0 %copy-start = (bf16[128,1024]{1,0:T(8,128)(2,1)S(1)}, bf16[128,1024]{1,0:T(8,128)(2,1)}, u32[]{:S(2)}) copy-start(bf16[128,1024]{1,0:T(8,128)(2,1)} %get-tuple-element.8) | copy-start | bytes 786436

commit v2 on v1

v2 whole, which is shorter than its diff:
```python
import functools
import math

import jax
import jax.numpy as jnp
from jax import lax
from jax.experimental import pallas as pl
from jax.experimental.pallas import tpu as pltpu
from jax.sharding import PartitionSpec as P

HEADS = 16
DH = 64
TILE = 128
MAXNB = 6
MASKED = -1e30
MESH = pl.DeviceIdType.MESH
EXPONENT = DH ** (-0.5) * math.log2(math.e)
NT = (((1,), (1,)), ((), ()))


def sweep(step, n):
    lax.fori_loop(1, n, step, 0)


def kernel(
    sections,
    tiles,
    near_ref,
    count_ref,
    q_ref,
    k_ref,
    v_ref,
    u_ref,
    dq_got,
    dk_got,
    dv_got,
    q_in,
    k_in,
    v_in,
    u_in,
    q_send,
    k_send,
    v_send,
    u_send,
    q_got,
    k_got,
    v_got,
    u_got,
    k_rows,
    v_rows,
    ds_all,
    pr_all,
    dq_send,
    dk_send,
    dv_send,
    p_all,
    slot_ref,
    load_sem,
    send_sem,
    recv_sem,
    q_sem,
    u_sem,
):
    section = lax.axis_index("section")
    me = lax.axis_index("seq")
    group = me // HEADS
    head = me % HEADS
    behind = lax.rem(section + sections - 1, sections)
    ahead = lax.rem(section + 1, sections)
    pairs = HEADS * MAXNB

    loads = [
        pltpu.make_async_copy(src, dst, load_sem.at[i])
        for i, (src, dst) in enumerate(
            ((k_ref, k_in), (q_ref, q_in), (v_ref, v_in), (u_ref, u_in))
        )
    ]
    for load in loads:
        load.start()
    barrier = pltpu.get_barrier_semaphore()

    def greet(r, c):
        pl.semaphore_signal(
            barrier, inc=1, device_id=(section, lax.rem(me + r, tiles)), device_id_type=MESH
        )
        return c

    def greet_ahead(h, c):
        pl.semaphore_signal(
            barrier, inc=1, device_id=(ahead, group * HEADS + h), device_id_type=MESH
        )
        return c

    lax.fori_loop(1, tiles, greet, 0)
    lax.fori_loop(0, HEADS, greet_ahead, 0)

    def turn(src, dst):
        for c in range(HEADS // 2):
            flipped = src[:, c * 128 : (c + 1) * 128].T
            dst[2 * c] = flipped[:DH]
            dst[2 * c + 1] = flipped[DH:]

    loads[0].wait()
    turn(k_in, k_send)
    loads[1].wait()
    turn(q_in, q_send)
    pl.semaphore_wait(barrier, tiles - 1 + HEADS)

    def remote(src, dst, sent, got, where, peer):
        return pltpu.make_async_remote_copy(
            src_ref=src,
            dst_ref=dst,
            send_sem=sent,
            recv_sem=got,
            device_id=(where, peer),
            device_id_type=MESH,
        )

    def send_keys(buffer, landing, index):
        def step(r, c):
            peer = lax.rem(me + r, tiles)
            remote(
                buffer.at[peer % HEADS],
                landing.at[me],
                send_sem.at[index],
                recv_sem.at[index],
                section,
                peer,
            ).start()
            return c

        sweep(step, tiles)

    def send_queries(buffer, landing, index, sem, where, first):
        def step(r, c):
            h = lax.rem(head + r, HEADS)
            remote(
                buffer.at[h],
                landing.at[head],
                send_sem.at[index],
                sem.at[head],
                where,
                group * HEADS + h,
            ).start()
            return c

        if first == 0:
            step(0, 0)
        sweep(step, HEADS)

    send_keys(k_send, k_got, 0)
    send_queries(q_send, q_got, 2, q_sem, section, 1)
    loads[2].wait()
    turn(v_in, v_send)
    send_keys(v_send, v_got, 1)
    loads[3].wait()
    turn(u_in, u_send)
    send_queries(u_send, u_got, 3, u_sem, behind, 0)
    k_got[me] = k_send[head]
    v_got[me] = v_send[head]
    q_got[head] = q_send[head]
    ds_all[pairs] = jnp.zeros((TILE, TILE), jnp.bfloat16)
    pr_all[pairs] = jnp.zeros((TILE, TILE), jnp.bfloat16)

    def find(a, c):
        tile = group * HEADS + a
        live = count_ref[tile]
        listed = [
            jnp.where(s < live, near_ref[s, tile], -1) for s in range(MAXNB)
        ]

        def one(b, c):
            found = jnp.int32(pairs)
            for s in range(MAXNB):
                found = jnp.where(listed[s] == b, a * MAXNB + s, found)
            slot_ref[b, a] = found
            return c

        return lax.fori_loop(0, tiles, one, c)

    lax.fori_loop(0, HEADS, find, 0)

    def settle(buffer, count, semaphore):
        part = buffer.at[pl.ds(0, count)]
        pltpu.make_async_copy(part, part, semaphore).wait()

    def upright(src, dst):
        def step(b, c):
            dst[b] = src[b].T
            return c

        lax.fori_loop(0, tiles, step, 0)

    settle(k_got, tiles - 1, recv_sem.at[0])
    upright(k_got, k_rows)

    def weigh(a):
        tile = group * HEADS + a
        live = count_ref[tile]
        query = q_got[a]
        scores = []
        for s in range(MAXNB):
            raw = jnp.dot(
                k_rows[near_ref[s, tile]], query, preferred_element_type=jnp.float32
            )
            scores.append(jnp.where(s < live, raw, MASKED) if s else raw)
        peak = functools.reduce(
            jnp.maximum, [jnp.max(raw, axis=0, keepdims=True) for raw in scores]
        )
        weights = [jnp.exp2((raw - peak) * EXPONENT) for raw in scores]
        share = 1.0 / sum(jnp.sum(w, axis=0, keepdims=True) for w in weights)
        for s in range(MAXNB):
            prob = weights[s] * share
            p_all[a * MAXNB + s] = prob
            pr_all[a * MAXNB + s] = prob.astype(jnp.bfloat16)

    def weigh_step(r, c):
        a = lax.rem(head + HEADS - r, HEADS)
        pltpu.make_async_copy(q_got.at[a], q_got.at[a], q_sem.at[a]).wait()
        weigh(a)
        return c

    weigh(head)
    lax.fori_loop(1, HEADS, weigh_step, 0)
    settle(v_got, tiles - 1, recv_sem.at[1])
    upright(v_got, v_rows)

    def query_tile(a):
        tile = group * HEADS + a
        pltpu.make_async_copy(u_got.at[a], u_got.at[a], u_sem.at[a]).wait()
        adjoint = u_got[a]
        near = [near_ref[s, tile] for s in range(MAXNB)]
        probs = [p_all[a * MAXNB + s] for s in range(MAXNB)]
        dprobs = [
            jnp.dot(v_rows[near[s]], adjoint, preferred_element_type=jnp.float32)
            for s in range(MAXNB)
        ]
        delta = sum(
            jnp.sum(p * d, axis=0, keepdims=True) for p, d in zip(probs, dprobs)
        )
        out = jnp.zeros((DH, TILE), jnp.float32)
        for s in range(MAXNB):
            dscore = (probs[s] * (dprobs[s] - delta) * (DH ** (-0.5))).astype(jnp.bfloat16)
            ds_all[a * MAXNB + s] = dscore
            out += jnp.dot(k_got[near[s]], dscore, preferred_element_type=jnp.float32)
        dq_send[a] = out.astype(jnp.bfloat16)

    query_tile(head)

    def query_step(r, c):
        a = lax.rem(head + HEADS - r, HEADS)
        query_tile(a)
        remote(
            dq_send.at[a],
            dq_got.at[head],
            send_sem.at[4],
            recv_sem.at[2],
            section,
            group * HEADS + a,
        ).start()
        return c

    lax.fori_loop(1, HEADS, query_step, 0)

    def key_tile(b):
        key_sum = jnp.zeros((DH, TILE), jnp.float32)
        value_sum = jnp.zeros((DH, TILE), jnp.float32)
        for a in range(HEADS):
            slot = slot_ref[b, a]
            key_sum += lax.dot_general(
                q_got[a], ds_all[slot], NT, preferred_element_type=jnp.float32
            )
            value_sum += lax.dot_general(
                u_got[a], pr_all[slot], NT, preferred_element_type=jnp.float32
            )
        dk_send[b] = key_sum.astype(jnp.bfloat16)
        dv_send[b] = value_sum.astype(jnp.bfloat16)

    def key_step(r, c):
        b = lax.rem(me + r, tiles)
        key_tile(b)
        remote(
            dk_send.at[b], dk_got.at[me], send_sem.at[5], recv_sem.at[3], section, b
        ).start()
        remote(
            dv_send.at[b], dv_got.at[me], send_sem.at[6], recv_sem.at[4], section, b
        ).start()
        return c

    sweep(key_step, tiles)
    key_tile(me)
    own = [
        pltpu.make_async_copy(src.at[i], dst.at[i], load_sem.at[n])
        for n, (src, dst, i) in enumerate(
            ((dq_send, dq_got, head), (dk_send, dk_got, me), (dv_send, dv_got, me))
        )
    ]
    for copy in own:
        copy.start()
    for copy in own:
        copy.wait()

    settle(dq_got, HEADS - 1, recv_sem.at[2])
    settle(dk_got, tiles - 1, recv_sem.at[3])
    settle(dv_got, tiles - 1, recv_sem.at[4])
    settle(k_got, tiles - 1, send_sem.at[0])
    settle(v_got, tiles - 1, send_sem.at[1])
    settle(q_got, HEADS - 1, send_sem.at[2])
    settle(u_got, HEADS, send_sem.at[3])
    settle(dq_got, HEADS - 1, send_sem.at[4])
    settle(dk_got, tiles - 1, send_sem.at[5])
    settle(dv_got, tiles - 1, send_sem.at[6])


def unturn(groups, dq_got, dk_got, dv_got, dq_ref, dk_ref, dv_ref, dq, dk, dv, turned, in_sem, out_sem):
    arrays = ((dq_got, dq, dq_ref), (dk_got, dk, dk_ref), (dv_got, dv, dv_ref))
    loads = [
        pltpu.make_async_copy(src, buffer, in_sem.at[n])
        for n, (src, buffer, dst) in enumerate(arrays)
    ]
    for load in loads:
        load.start()
    stores = []
    for n, (src, buffer, dst) in enumerate(arrays):
        loads[n].wait()
        for c in range(HEADS // 2):
            pair = buffer[2 * c : 2 * c + 2]
            if n and groups > 1:
                pair = sum(
                    buffer[g * HEADS + 2 * c : g * HEADS + 2 * c + 2].astype(jnp.float32)
                    for g in range(groups)
                ).astype(jnp.bfloat16)
            turned[n, :, c * 128 : (c + 1) * 128] = pair.reshape(TILE, TILE).T
        stores.append(pltpu.make_async_copy(turned.at[n], dst, out_sem.at[n]))
        stores[n].start()
    for store in stores:
        store.wait()


def per_device(queries, keys, values, upstream, neighbours, counts):
    sections = lax.axis_size("section")
    tiles = lax.axis_size("seq")
    rows, width = queries.shape[1:]
    assert rows == TILE and width == HEADS * DH and tiles % HEADS == 0
    smem = pl.BlockSpec(memory_space=pltpu.SMEM)
    out = jax.ShapeDtypeStruct((rows, width), jnp.bfloat16)

    def blocks(count):
        return pltpu.VMEM((count, DH, TILE), jnp.bfloat16)

    pairs = HEADS * MAXNB + 1
    whole = pl.BlockSpec(memory_space=pl.ANY)

    def shape(count):
        return jax.ShapeDtypeStruct((count, DH, TILE), jnp.bfloat16)

    got = pl.pallas_call(
        functools.partial(kernel, sections, tiles),
        out_shape=(shape(HEADS), shape(tiles), shape(tiles)),
        in_specs=[smem, smem, whole, whole, whole, whole],
        out_specs=(whole,) * 3,
        scratch_shapes=[pltpu.VMEM((rows, width), jnp.bfloat16)] * 4
        + [blocks(HEADS)] * 4
        + [blocks(HEADS), blocks(tiles), blocks(tiles), blocks(HEADS)]
        + [pltpu.VMEM((tiles, TILE, DH), jnp.bfloat16)] * 2
        + [pltpu.VMEM((pairs, TILE, TILE), jnp.bfloat16)] * 2
        + [blocks(HEADS), blocks(tiles), blocks(tiles)]
        + [pltpu.VMEM((pairs, TILE, TILE), jnp.float32)]
        + [
            pltpu.SMEM((tiles, HEADS), jnp.int32),
            pltpu.SemaphoreType.DMA((4,)),
            pltpu.SemaphoreType.DMA((7,)),
            pltpu.SemaphoreType.DMA((5,)),
            pltpu.SemaphoreType.DMA((HEADS,)),
            pltpu.SemaphoreType.DMA((HEADS,)),
        ],
        compiler_params=pltpu.CompilerParams(
            collective_id=0, has_side_effects=True, vmem_limit_bytes=60 * 1024 * 1024
        ),
    )(neighbours.T, counts, queries[0], keys[0], values[0], upstream[0])
    dq, dk, dv = pl.pallas_call(
        functools.partial(unturn, tiles // HEADS),
        out_shape=(out, out, out),
        in_specs=[whole] * 3,
        out_specs=(whole, whole, whole),
        scratch_shapes=[
            blocks(HEADS),
            blocks(tiles),
            blocks(tiles),
            pltpu.VMEM((3, rows, width), jnp.bfloat16),
            pltpu.SemaphoreType.DMA((3,)),
            pltpu.SemaphoreType.DMA((3,)),
        ],
    )(*got)
    return dq[None], dk[None], dv[None]


def solution(mesh):
    spec = P("section", "seq", None)
    return jax.shard_map(
        per_device,
        mesh=mesh,
        in_specs=(spec, spec, spec, spec, P(), P()),
        out_specs=(spec, spec, spec),
        check_vma=False,
    )
```

time: 61 us -> 55.9 us (0.916)
  local copies, waits for them, and re-layouts: 4.82 us -> 0 us
    unnamed x10 -> x0, local copies, waits for them, and re-layouts: 4.82 us -> none
    pallas_call x1 -> x2, Pallas kernels: 55 us -> 55 us  [the longest x1 53 us: per_device(): pl.pallas_call(functools.partial(kernel, sections, tiles), out_shape=(sha...]
where the time goes in v2:
time: 55.9 us; the launch traced here: 55.7 us
  Pallas kernels  55 us (98%)
  between operations  0.64 us (1%)
    pallas_call x1, Pallas kernels, per_device(): pl.pallas_call(functools.partial(kernel, sections, tiles), out_shape=(sha...  53 us
    pallas_call x1, Pallas kernels, per_device(): pl.pallas_call(functools.partial(unturn, tiles // HEADS), out_shape=(out,...  2.07 us

profile of v2, /device:TPU:11, one launch (start us, length us, event | category | flops | bytes accessed | tf_op | source)
XLA Modules:
  0.0 55.7 jit_solution(16890948036185089423)
XLA Ops:
  0.6 53.0 %shard_map.85 = (bf16[16,64,128]{2,1,0:T(8,128)(2,1)}, bf16[16,64,128]{2,1,0:T(8,128)(2,1)}, bf16[16,64,128]{2,1,0:T(8,128)(2,1)}) custom-call(s32[6,16]{1,0:T(8,128)} %bitcast.12, s32[16]{0:T(128)} %count_ref.1, bf16[128,1024]{1,0:T(8,128)(2,1)} %bitcast.8, bf16[128,1024]{1,0:T(8,128)(2,1)} %bitcast.9, bf16[128,1024]{1,0:T(8,128)(2,1)} %bitcast.10, ...), custom_call_target="tpu_custom_call" | custom-call | tf_op jit(solution)/shard_map/pallas_call | solution.py:357
  53.6 2.1 %shard_map.86 = (bf16[128,1024]{1,0:T(8,128)(2,1)}, bf16[128,1024]{1,0:T(8,128)(2,1)}, bf16[128,1024]{1,0:T(8,128)(2,1)}) custom-call(bf16[16,64,128]{2,1,0:T(8,128)(2,1)} %get-tuple-element.9.dq_got, bf16[16,64,128]{2,1,0:T(8,128)(2,1)} %get-tuple-element.10.dk_got, bf16[16,64,128]{2,1,0:T(8,128)(2,1)} %get-tuple-element.11.dv_got), custom_call_target="tpu_custom_call" | custom-call | tf_op jit(solution)/shard_map/pallas_call | solution.py:381

commit v3 on v2

--- a/solution.py
+++ b/solution.py
@@ -18,8 +18,8 @@
 NT = (((1,), (1,)), ((), ()))
 
 
-def sweep(step, n):
-    lax.fori_loop(1, n, step, 0)
+def sweep(step, n, first=0):
+    lax.fori_loop(0, n - 1, lambda r, c: step(lax.rem(r + first, n - 1) + 1, c), 0)
 
 
 def kernel(
@@ -131,7 +131,7 @@
 
         sweep(step, tiles)
 
-    def send_queries(buffer, landing, index, sem, where, first):
+    def send_queries(buffer, landing, index, sem, where, first, turn_at):
         def step(r, c):
             h = lax.rem(head + r, HEADS)
             remote(
@@ -146,16 +146,16 @@
 
         if first == 0:
             step(0, 0)
-        sweep(step, HEADS)
+        sweep(step, HEADS, turn_at)
 
     send_keys(k_send, k_got, 0)
-    send_queries(q_send, q_got, 2, q_sem, section, 1)
+    send_queries(q_send, q_got, 2, q_sem, section, 1, 0)
     loads[2].wait()
     turn(v_in, v_send)
     send_keys(v_send, v_got, 1)
     loads[3].wait()
     turn(u_in, u_send)
-    send_queries(u_send, u_got, 3, u_sem, behind, 0)
+    send_queries(u_send, u_got, 3, u_sem, behind, 0, HEADS // 2 - 1)
     k_got[me] = k_send[head]
     v_got[me] = v_send[head]
     q_got[head] = q_send[head]
@@ -221,7 +221,7 @@
         return c
 
     weigh(head)
-    lax.fori_loop(1, HEADS, weigh_step, 0)
+    sweep(weigh_step, HEADS)
     settle(v_got, tiles - 1, recv_sem.at[1])
     upright(v_got, v_rows)
 
@@ -260,7 +260,7 @@
         ).start()
         return c
 
-    lax.fori_loop(1, HEADS, query_step, 0)
+    sweep(query_step, HEADS, HEADS // 2 - 1)
 
     def key_tile(b):
         key_sum = jnp.zeros((DH, TILE), jnp.float32)

time: 55.9 us -> 55.9 us (level)
  no operation moved by 1% of the time
where the time goes in v3:
time: 55.9 us; the launch traced here: 55.7 us
  Pallas kernels  55 us (98%)
  between operations  0.64 us (1%)
    pallas_call x1, Pallas kernels, per_device(): pl.pallas_call(functools.partial(kernel, sections, tiles), out_shape=(sha...  53 us
    pallas_call x1, Pallas kernels, per_device(): pl.pallas_call(functools.partial(unturn, tiles // HEADS), out_shape=(out,...  2.07 us

profile of v3, /device:TPU:11, one launch (start us, length us, event | category | flops | bytes accessed | tf_op | source)
XLA Modules:
  0.0 55.7 jit_solution(6146295710058116560)
XLA Ops:
  0.6 53.0 %shard_map.85 = (bf16[16,64,128]{2,1,0:T(8,128)(2,1)}, bf16[16,64,128]{2,1,0:T(8,128)(2,1)}, bf16[16,64,128]{2,1,0:T(8,128)(2,1)}) custom-call(s32[6,16]{1,0:T(8,128)} %bitcast.12, s32[16]{0:T(128)} %count_ref.1, bf16[128,1024]{1,0:T(8,128)(2,1)} %bitcast.8, bf16[128,1024]{1,0:T(8,128)(2,1)} %bitcast.9, bf16[128,1024]{1,0:T(8,128)(2,1)} %bitcast.10, ...), custom_call_target="tpu_custom_call" | custom-call | tf_op jit(solution)/shard_map/pallas_call | solution.py:357
  53.6 2.1 %shard_map.86 = (bf16[128,1024]{1,0:T(8,128)(2,1)}, bf16[128,1024]{1,0:T(8,128)(2,1)}, bf16[128,1024]{1,0:T(8,128)(2,1)}) custom-call(bf16[16,64,128]{2,1,0:T(8,128)(2,1)} %get-tuple-element.9.dq_got, bf16[16,64,128]{2,1,0:T(8,128)(2,1)} %get-tuple-element.10.dk_got, bf16[16,64,128]{2,1,0:T(8,128)(2,1)} %get-tuple-element.11.dv_got), custom_call_target="tpu_custom_call" | custom-call | tf_op jit(solution)/shard_map/pallas_call | solution.py:381
